TPU v7x, 128 devices: a whole 4x4x4 slice. The times are simulated.
128 devices in a mesh: section: 2 (over z_hi), seq: 8 (over x, z_lo), expert: 8 (over y, core).
Axes of the slice: x: 4, y: 4, z: 4 (z_hi: 2, z_lo: 2; z = z_hi * 2 + z_lo), core: 2. Of those that a mesh axis runs over, the one named last changes fastest.
Arguments:
- tokens: bfloat16 [2, 1024, 2048], P(None, ('seq', 'expert')), may hold values from -12 to 12
- prompt_lengths: int32 [2, 3], replicated, may hold values from 1 to 512, 1024 in all within a row
- cache_lengths: int32 [2, 3], replicated, may hold values from 1 to 1024, 2048 in all within a row
- kv_cache: bfloat16 [2, 2048, 2, 2048], P(None, 'seq', None, 'expert'), may hold values from -360 to 360
- attn_routes: int32 [2, 1024, 2], P(None, 'seq'), may hold values from 0 to 3, all different within a row
- ffn_routes: int32 [2, 1024, 2], P(None, ('seq', 'expert')), may hold values from 0 to 7, all different within a row; in each aligned block of 16 rows (0 to 15, 16 to 31, ..., all dimensions but the last counted through in order) at most 8 rows name the same one
- attn_gain: float32 [2048], replicated, may hold values from 0.1 to 1.9
- ffn_gain: float32 [2048], replicated, may hold values from 0.1 to 1.9
- attn_mix: bfloat16 [2048, 4], replicated, may hold values from -0.125 to 0.125
- query_weight: bfloat16 [2048, 4, 2048], P(None, None, 'expert'), may hold values from -0.125 to 0.125
- kv_weight: bfloat16 [2048, 2, 2048], P(None, None, 'expert'), may hold values from -0.125 to 0.125
- out_weight: bfloat16 [4, 2048, 2048], P(None, 'expert'), may hold values from -0.125 to 0.125
- ffn_mix: bfloat16 [2048, 8], replicated, may hold values from -0.125 to 0.125
- in_weight: bfloat16 [8, 2048, 2, 5632], P('expert', None, None, 'seq'), may hold values from -0.125 to 0.125
- down_weight: bfloat16 [8, 5632, 2048], P('expert', 'seq'), may hold values from -0.078125 to 0.078125
Outputs:
- layer_out: bfloat16 [2, 1024, 2048], P('section', ('seq', 'expert'))
Inputs may be any that keep to these rules, and one draw needn't show every extreme that they name: `prompt_lengths`: each row sums to 1024; its largest entry is 512. `cache_lengths`: each row sums to 2048; its largest entry is 1024. `attn_routes`: the two experts of a position differ; every expert is named somewhere. `ffn_routes`: the two experts of a position differ. Taking all micro-batches and positions in order, in each aligned block of 16 positions (the rows of one device) no expert is named more than 8 times, and some block names one exactly 8 times.
All inputs are finite; a program needn't handle non-finite values.
Results may differ from a plain program's by a relative error of at most 0.029.
Values may be sent and summed in bfloat16 or wider, within the bound.
A program may use at most 128 MiB of HBM per device.

v0:
```python
import jax
import jax.numpy as jnp
from jax import lax
from jax.sharding import PartitionSpec as P

HEAD_DIM = 128
EPS = 1e-06
THETA = 10000.0
NEGATIVE = -1e30


def rms_scale(values, gain):
    widened = values.astype(jnp.float32)
    inverse = lax.rsqrt(jnp.mean(widened * widened, axis=-1, keepdims=True) + EPS)
    return (widened * inverse * gain).astype(jnp.bfloat16)


def segment_of(row_index, lengths):
    ends = jnp.cumsum(lengths)
    return jnp.sum((row_index[:, None] >= ends[None, :]).astype(jnp.int32), axis=1)


def positions(row_index, lengths, cached):
    ends = jnp.cumsum(lengths)
    segment = jnp.sum((row_index[:, None] >= ends[None, :]).astype(jnp.int32), axis=1)
    matched = segment[:, None] == jnp.arange(lengths.shape[0], dtype=jnp.int32)[None, :]
    begins = jnp.sum(jnp.where(matched, (ends - lengths)[None, :], 0), axis=1)
    offsets = jnp.sum(jnp.where(matched, cached[None, :], 0), axis=1)
    return (segment, offsets + row_index - begins)


def rotate(values, place):
    half_dim = values.shape[-1] // 2
    freq = THETA ** (-jnp.arange(half_dim, dtype=jnp.float32) / half_dim)
    angle = place.astype(jnp.float32)[:, None] * freq[None, :]
    shape = (values.shape[0],) + (1,) * (values.ndim - 2) + (half_dim,)
    cosine = jnp.cos(angle).reshape(shape)
    sine = jnp.sin(angle).reshape(shape)
    former = values[..., :half_dim]
    latter = values[..., half_dim:]
    return jnp.concatenate(
        [former * cosine - latter * sine, latter * cosine + former * sine], axis=-1
    )


def route_gates(normed, mixing, routes):
    logits = jnp.dot(normed, mixing, preferred_element_type=jnp.float32)
    chosen = jnp.take_along_axis(logits, routes, axis=1)
    leading = jax.nn.sigmoid(chosen[:, 0] - chosen[:, 1])
    return jnp.stack([leading, 1.0 - leading], axis=1)


def select_batch(values, batch):
    return lax.dynamic_index_in_dim(values, batch, 0, keepdims=False)


def attention_block(
    own_rows, lengths, cached, cache_rows, routes, gain, mixing, query_weight, kv_weight, out_weight
):
    gathered = lax.all_gather(own_rows, "expert", axis=0, tiled=True)
    count = gathered.shape[0]
    normed = rms_scale(gathered, gain)
    row_index = lax.axis_index("seq") * count + jnp.arange(count, dtype=jnp.int32)
    segment, place = positions(row_index, lengths, cached)
    gates = route_gates(normed, mixing, routes)
    experts = query_weight.shape[1]
    width = query_weight.shape[2]
    local_heads = width // HEAD_DIM
    query_all = jnp.dot(
        normed, query_weight.reshape(query_weight.shape[0], -1), preferred_element_type=jnp.float32
    )
    query_all = query_all.reshape(count, experts, local_heads, HEAD_DIM)
    query = jnp.take_along_axis(query_all, routes[:, :, None, None], axis=1)
    query = rotate(query, place).astype(jnp.bfloat16)
    queries = query.reshape(count * 2, local_heads, HEAD_DIM)
    projected = jnp.dot(
        normed, kv_weight.reshape(kv_weight.shape[0], -1), preferred_element_type=jnp.float32
    )
    projected = projected.reshape(count, 2, local_heads, HEAD_DIM)
    fresh_keys = rotate(projected[:, 0], place).astype(jnp.bfloat16).reshape(count, width)
    fresh_values = projected[:, 1].astype(jnp.bfloat16).reshape(count, width)
    fresh = jnp.stack([fresh_keys, fresh_values], axis=1)
    query_segment = jnp.repeat(segment, 2)
    query_index = jnp.repeat(row_index, 2)
    scale = HEAD_DIM ** (-0.5)
    slots = count * 2

    def absorb(carried, piece, allowed):
        row_top, row_total, row_sum = carried
        keys = piece[:, 0].reshape(-1, local_heads, HEAD_DIM)
        values = piece[:, 1].reshape(-1, local_heads, HEAD_DIM)
        scores = (
            jnp.einsum("qhd,khd->hqk", queries, keys, preferred_element_type=jnp.float32) * scale
        )
        scores = jnp.where(allowed[None], scores, NEGATIVE)
        new_top = jnp.maximum(row_top, jnp.max(scores, axis=2))
        weights = jnp.where(allowed[None], jnp.exp(scores - new_top[:, :, None]), 0.0)
        shrink = jnp.exp(row_top - new_top)
        row_total = row_total * shrink + jnp.sum(weights, axis=2)
        row_sum = row_sum * shrink[:, :, None] + jnp.einsum(
            "hqk,khd->hqd", weights.astype(jnp.bfloat16), values, preferred_element_type=jnp.float32
        )
        return (new_top, row_total, row_sum)

    initial = (
        jnp.full((local_heads, slots), NEGATIVE, jnp.float32),
        jnp.zeros((local_heads, slots), jnp.float32),
        jnp.zeros((local_heads, slots, HEAD_DIM), jnp.float32),
    )
    piece = lax.all_gather(cache_rows, "seq", axis=0, tiled=True)
    key_segment = segment_of(jnp.arange(piece.shape[0], dtype=jnp.int32), cached)
    allowed = query_segment[:, None] == key_segment[None, :]
    carried = absorb(initial, piece, allowed)
    piece = lax.all_gather(fresh, "seq", axis=0, tiled=True)
    key_index = jnp.arange(piece.shape[0], dtype=jnp.int32)
    key_segment = segment_of(key_index, lengths)
    allowed = (query_segment[:, None] == key_segment[None, :]) & (
        key_index[None, :] <= query_index[:, None]
    )
    row_top, row_total, row_sum = absorb(carried, piece, allowed)
    attended = (row_sum / row_total[:, :, None]).astype(jnp.bfloat16)
    attended = attended.transpose(1, 0, 2).reshape(count, 2, width)
    select = (routes[:, :, None] == jnp.arange(experts, dtype=jnp.int32)[None, None, :]).astype(
        jnp.float32
    )
    select = select * gates[:, :, None]
    spread = jnp.einsum("tka,tkd->tad", select, attended.astype(jnp.float32)).astype(jnp.bfloat16)
    spread = spread.reshape(count, experts * width)
    out_flat = out_weight.reshape(experts * width, -1)
    term = lax.psum_scatter(
        jnp.dot(spread, out_flat, preferred_element_type=jnp.float32).astype(jnp.bfloat16),
        "expert",
        scatter_dimension=0,
        tiled=True,
    ).astype(jnp.float32)
    return (own_rows.astype(jnp.float32) + term).astype(jnp.bfloat16)


def expert_hidden(rows, in_weight):
    single = in_weight[0]
    both = jnp.dot(rows, single.reshape(single.shape[0], -1), preferred_element_type=jnp.float32)
    both = both.reshape(rows.shape[0], 2, -1)
    return (jax.nn.silu(both[:, 0]) * both[:, 1]).astype(jnp.bfloat16)


def expert_block(middle, routes, gain, mixing, in_weight, down_weight):
    rows = middle.shape[0]
    features = middle.shape[1]
    normed = rms_scale(middle, gain)
    gates = route_gates(normed, mixing, routes)
    experts = mixing.shape[1]
    capacity = max(2, 4 * rows // experts)
    flat = routes.reshape(-1)
    member = (flat[:, None] == jnp.arange(experts, dtype=jnp.int32)[None, :]).astype(jnp.int32)
    earlier = jnp.cumsum(member, axis=0) - member
    slot = jnp.sum(earlier * member, axis=1)
    target = flat * capacity + slot
    table = (jnp.arange(experts * capacity, dtype=jnp.int32)[:, None] == target[None, :]).astype(
        jnp.bfloat16
    )
    table = jnp.sum(table.reshape(experts * capacity, rows, 2), axis=2)
    buffer = jnp.dot(table, normed, preferred_element_type=jnp.float32).astype(jnp.bfloat16)
    buffer = buffer.reshape(experts, capacity, features)
    seq_count = lax.axis_size("seq")
    copies = jnp.broadcast_to(buffer[None], (seq_count,) + buffer.shape)
    copies = copies.reshape(seq_count * experts, capacity, features)
    arrived = lax.all_to_all(copies, ("seq", "expert"), split_axis=0, concat_axis=0, tiled=True)
    flat_rows = arrived.reshape(-1, features)
    hidden = expert_hidden(flat_rows, in_weight)
    partial_value = jnp.dot(hidden, down_weight[0], preferred_element_type=jnp.float32)
    partial_value = partial_value.astype(jnp.bfloat16).reshape(arrived.shape)
    returned = lax.all_to_all(
        partial_value, ("seq", "expert"), split_axis=0, concat_axis=0, tiled=True
    )
    results = jnp.sum(
        returned.reshape(seq_count, experts, capacity, features).astype(jnp.float32), axis=0
    )
    picked = jnp.take(results.reshape(experts * capacity, features), target, axis=0).reshape(
        rows, 2, features
    )
    mixture = gates[:, 0:1] * picked[:, 0] + gates[:, 1:2] * picked[:, 1]
    return (middle.astype(jnp.float32) + mixture).astype(jnp.bfloat16)


def on_device(
    tokens,
    prompt_lengths,
    cache_lengths,
    kv_cache,
    attn_routes,
    ffn_routes,
    attn_gain,
    ffn_gain,
    attn_mix,
    query_weight,
    kv_weight,
    out_weight,
    ffn_mix,
    in_weight,
    down_weight,
):
    batch = lax.axis_index("section")
    middle = attention_block(
        select_batch(tokens, batch),
        select_batch(prompt_lengths, batch),
        select_batch(cache_lengths, batch),
        select_batch(kv_cache, batch),
        select_batch(attn_routes, batch),
        attn_gain,
        attn_mix,
        query_weight,
        kv_weight,
        out_weight,
    )
    finished = expert_block(
        middle, select_batch(ffn_routes, batch), ffn_gain, ffn_mix, in_weight, down_weight
    )
    return finished[None]


def solution(mesh):
    return jax.shard_map(
        on_device,
        mesh=mesh,
        in_specs=(
            P(None, ("seq", "expert"), None),
            P(),
            P(),
            P(None, "seq", None, "expert"),
            P(None, "seq", None),
            P(None, ("seq", "expert"), None),
            P(),
            P(),
            P(),
            P(None, None, "expert"),
            P(None, None, "expert"),
            P(None, "expert", None),
            P(),
            P("expert", None, None, "seq"),
            P("expert", "seq", None),
        ),
        out_specs=P("section", ("seq", "expert"), None),
        check_vma=False,
    )
```

profile of v0, /device:TPU:1, one launch (start us, length us, event | category | flops | bytes accessed | tf_op | source)
XLA Modules:
  0.0 283.1 jit_solution(11401811092933586299)
XLA Ops:
  8.2 15.0 %all-gather = bf16[1,128,2048]{2,1,0:T(8,128)(2,1)S(1)} all-gather(bf16[1,16,2048]{2,1,0:T(8,128)(2,1)S(1)} %constant_dynamic-slice_fusion.5), channel_id=2, replica_groups=mesh['section'=2,'seq'=8,'expert'=8] {'expert'}, dimensions={1}, use_global_device_ids=true | all-gather | bytes 589824 | tf_op jit(solution)/shard_map/all_gather | solution.py:60
  23.3 3.4 %copy.115 = bf16[256,8,2,256]{3,1,2,0:T(8,128)(2,1)} copy(bf16[256,8,2,256]{3,2,1,0:T(2,128)(2,1)} %bitcast.189) | data formatting | bytes 4194304
  26.7 4.0 %copy.97 = bf16[512,2048]{1,0:T(8,128)(2,1)} copy(bf16[512,2048]{0,1:T(8,128)(2,1)} %bitcast.186) | data formatting | bytes 4194304 | tf_op jit(solution)/shard_map/dot_general | solution.py:76
  30.7 2.4 fusion.42
  41.0 1.8 constant_dynamic-slice_fusion.1
  42.8 1.8 copy.113
  48.3 2.4 gather_fusion.1
  51.0 5.2 %copy.114 = bf16[256,8,4,256]{3,1,2,0:T(8,128)(2,1)} copy(bf16[256,8,4,256]{3,2,1,0:T(4,128)(2,1)} %bitcast.187) | data formatting | bytes 8388608
  56.2 6.5 %copy.89 = bf16[1024,2048]{1,0:T(8,128)(2,1)} copy(bf16[1024,2048]{0,1:T(8,128)(2,1)} %bitcast.183) | data formatting | bytes 8388608 | tf_op jit(solution)/shard_map/dot_general | solution.py:69
  62.7 3.7 %fusion.44 = f32[128,4,2,128]{3,0,2,1:T(8,128)S(1)} fusion(bf16[4,2,128,2048]{3,2,1,0:T(8,128)(2,1)} %bitcast.182, bf16[1,128,2048]{2,1,0:T(8,128)(2,1)S(1)} %all-gather, f32[2048]{0:T(1024)S(1)} %copy-done.12, f32[128]{0:T(128)S(1)} %copy-done.23), kind=kOutput, calls=%fused_computation.52 | convolution fusion | flops 537919488 | bytes 5251584 | tf_op jit(solution)/shard_map/dot_general | solution.py:69
  66.9 1.9 gather_fusion.2
  73.4 2.0 subtract_convert_fusion
  75.7 5.5 %all-gather.5.cloned.1.call-done = bf16[1024,2,256]{0,2,1:T(8,128)(2,1)} async-done(((bf16[128,2,256]{0,2,1:T(8,128)(2,1)}), bf16[1024,2,256]{0,2,1:T(8,128)(2,1)}) %all-gather.5.cloned.1.call-update) | async-done | bytes 1048592 | tf_op jit(solution)/shard_map/all_gather | solution.py:114
  81.2 2.1 fusion.105
  83.3 2.0 fusion.15
  85.3 59.9 %all-gather.7.cloned.1.call-done = bf16[1,2048,2,256]{1,3,2,0:T(8,128)(2,1)} async-done(((bf16[1,256,2,256]{1,3,2,0:T(8,128)(2,1)}), bf16[1,2048,2,256]{1,3,2,0:T(8,128)(2,1)}) %all-gather.7.cloned.1.call-update) | async-done | bytes 2097168 | tf_op jit(solution)/shard_map/all_gather | solution.py:110
  154.0 3.7 %fusion.9 = bf16[128,2048]{1,0:T(8,128)(2,1)} fusion(bf16[4,256,2048]{2,1,0:T(8,128)(2,1)} %param.26, bf16[128,4,256]{2,1,0:T(4,128)(2,1)S(1)} %convolution_convert_fusion.2), kind=kOutput, calls=%fused_computation.16 | convolution fusion | flops 537133056 | bytes 4980736 | tf_op jit(solution)/shard_map/dot_general | solution.py:131
  158.7 30.2 %reduce-scatter.2.cloned.1.call-done = bf16[16,2048]{1,0:T(8,128)(2,1)} async-done(((bf16[128,2048]{1,0:T(8,128)(2,1)}), bf16[16,2048]{1,0:T(8,128)(2,1)}) %reduce-scatter.2.cloned.1.call-update) | async-done | bytes 65552 | tf_op jit(solution)/shard_map/reduce_scatter | solution.py:130
  190.4 38.1 %all_to_all.10 = bf16[64,8,2048]{2,1,0:T(8,128)(2,1)S(1)} all-to-all(bf16[64,8,2048]{2,1,0:T(8,128)(2,1)S(1)} %bitcast.185), channel_id=1, replica_groups=mesh['section'=2,'seq'=8,'expert'=8] {'seq','expert'}, dimensions={0} | all-to-all | bytes 4194304 | tf_op jit(solution)/shard_map/all_to_all | solution.py:167
  228.5 5.2 %fusion = f32[512,2,704]{0,2,1:T(8,128)S(1)} fusion(bf16[1,2048,2,704]{1,3,2,0:T(8,128)(2,1)} %param.28, bf16[64,8,2048]{2,1,0:T(8,128)(2,1)S(1)} %all_to_all.10), kind=kOutput, calls=%fused_computation.4 | convolution fusion | flops 2952790016 | bytes 10747904 | tf_op jit(solution)/shard_map/dot_general | solution.py:141
  233.7 3.3 %fusion.6 = bf16[64,8,2048]{2,1,0:T(8,128)(2,1)} fusion(bf16[1,704,2048]{2,1,0:T(8,128)(2,1)S(1)} %copy-done, f32[512,2,704]{0,2,1:T(8,128)S(1)} %fusion), kind=kOutput, calls=%fused_computation.14 | convolution fusion | flops 1479606272 | bytes 7864320 | tf_op jit(solution)/shard_map/dot_general | solution.py:170
  237.0 5.3 %all-to-all-start.1 = ((bf16[64,8,2048]{2,1,0:T(8,128)(2,1)}), bf16[64,8,2048]{2,1,0:T(8,128)(2,1)}, u32[]{:S(2)}, u32[]{:S(2)}) async-start(bf16[64,8,2048]{2,1,0:T(8,128)(2,1)} %fusion.6), calls=%async_computation.2 | async-start | bytes 4194304 | tf_op jit(solution)/shard_map/all_to_all | solution.py:172
  243.8 27.5 %all-to-all-done.1 = bf16[64,8,2048]{2,1,0:T(8,128)(2,1)} async-done(((bf16[64,8,2048]{2,1,0:T(8,128)(2,1)}), bf16[64,8,2048]{2,1,0:T(8,128)(2,1)}, u32[]{:S(2)}, u32[]{:S(2)}) %all-to-all-start.1) | async-done | bytes 2097184 | tf_op jit(solution)/shard_map/all_to_all | solution.py:172
  271.2 2.0 convert_reduce_fusion
  (144 shorter events, 34.7 us)
Async XLA Ops:
  6.5 227.2 %copy-start = (bf16[1,704,2048]{2,1,0:T(8,128)(2,1)S(1)}, bf16[1,704,2048]{2,1,0:T(8,128)(2,1)}, u32[]{:S(2)}) copy-start(bf16[1,704,2048]{2,1,0:T(8,128)(2,1)} %param.29) | copy-start | bytes 8650756
  6.5 74.7 %all-gather.5.cloned.1.call-start = ((), (), s32[]{:S(2)}) async-start(), calls=%async_computation.3 | async-start | bytes 1179648 | tf_op jit(solution)/shard_map/all_gather | solution.py:114
  23.3 7.4 %copy-start.22 = (f32[128]{0:T(128)}, f32[128]{0:T(128)S(1)}, u32[]{:S(2)}) copy-start(f32[128]{0:T(128)S(1)} %add_rsqrt_fusion.1) | copy-start | bytes 1540
  26.7 4.0 %copy-start.12 = (f32[2048]{0:T(1024)S(1)}, f32[2048]{0:T(1024)}, u32[]{:S(2)}) copy-start(f32[2048]{0:T(1024)} %param.21) | copy-start | bytes 24580
  30.7 3.1 %copy-start.17 = (s32[2,3]{1,0:T(2,128)S(1)}, s32[2,3]{1,0:T(2,128)}, u32[]{:S(2)}) copy-start(s32[2,3]{1,0:T(2,128)} %param.16) | copy-start | bytes 76
  30.7 3.1 %copy-start.24 = (s32[2,3]{1,0:T(2,128)S(1)}, s32[2,3]{1,0:T(2,128)}, u32[]{:S(2)}) copy-start(s32[2,3]{1,0:T(2,128)} %param.17) | copy-start | bytes 76
  33.1 14.6 %copy-start.14 = (s32[2,128,2]{1,2,0:T(2,128)S(1)}, s32[2,128,2]{1,2,0:T(2,128)}, u32[]{:S(2)}) copy-start(s32[2,128,2]{1,2,0:T(2,128)} %param.19) | copy-start | bytes 6148
  39.4 8.5 %copy-start.23 = (f32[128]{0:T(128)S(1)}, f32[128]{0:T(128)}, u32[]{:S(2)}) copy-start(f32[128]{0:T(128)} %copy-done.22) | copy-start | bytes 1540
  39.4 8.6 %copy-start.26 = (bf16[2048,4]{0,1:T(4,128)(2,1)S(1)}, bf16[2048,4]{0,1:T(4,128)(2,1)}, u32[]{:S(2)}) copy-start(bf16[2048,4]{0,1:T(4,128)(2,1)} %param.23) | copy-start | bytes 49156
  41.0 104.3 %all-gather.7.cloned.1.call-start = ((), (), s32[]{:S(2)}) async-start(), calls=%async_computation.5 | async-start | bytes 2359296 | tf_op jit(solution)/shard_map/all_gather | solution.py:110
  44.7 144.2 %reduce-scatter.2.cloned.1.call-start = ((), (), s32[]{:S(2)}) async-start(), calls=%async_computation.4 | async-start | bytes 589824 | tf_op jit(solution)/shard_map/reduce_scatter | solution.py:130
  62.7 6.3 %copy-start.19 = (s32[128]{0:T(128)S(1)}, s32[128]{0:T(128)}, u32[]{:S(2)}) copy-start(s32[128]{0:T(128)} %copy-done.18) | copy-start | bytes 1540
  62.7 6.6 %copy-start.21 = (s32[3,1]{0,1:T(1,128)S(1)}, s32[3,1]{0,1:T(1,128)}, u32[]{:S(2)}) copy-start(s32[3,1]{0,1:T(1,128)} %get-tuple-element.33) | copy-start | bytes 40
  62.7 8.2 %copy-start.16 = (s32[3,1]{0,1:T(1,128)S(1)}, s32[3,1]{0,1:T(1,128)}, u32[]{:S(2)}) copy-start(s32[3,1]{0,1:T(1,128)} %copy-done.15) | copy-start | bytes 40
  81.2 2.1 copy-start.2
  81.2 2.1 copy-start.4
  145.3 1.8 copy-start.5
  148.3 1.6 copy-start.1
  148.3 1.6 copy-start.3
  153.9 3.8 %copy-start.20 = (s32[2,16,2]{1,2,0:T(2,128)S(1)}, s32[2,16,2]{1,2,0:T(2,128)}, u32[]{:S(2)}) copy-start(s32[2,16,2]{1,2,0:T(2,128)} %param.20) | copy-start | bytes 772
  153.9 34.9 %copy-start.9 = (bf16[2,16,2048]{2,1,0:T(8,128)(2,1)S(1)}, bf16[2,16,2048]{2,1,0:T(8,128)(2,1)}, u32[]{:S(2)}) copy-start(bf16[2,16,2048]{2,1,0:T(8,128)(2,1)} %param.15) | copy-start | bytes 393220
  153.9 35.9 %copy-start.13 = (f32[2048]{0:T(1024)S(1)}, f32[2048]{0:T(1024)}, u32[]{:S(2)}) copy-start(f32[2048]{0:T(1024)} %param.22) | copy-start | bytes 24580
  237.0 5.7 %copy-start.25 = (bf16[2048,8]{0,1:T(8,128)(2,1)S(1)}, bf16[2048,8]{0,1:T(8,128)(2,1)}, u32[]{:S(2)}) copy-start(bf16[2048,8]{0,1:T(8,128)(2,1)} %param.27) | copy-start | bytes 98308
  237.0 34.2 %all-to-all-start.1 = ((bf16[64,8,2048]{2,1,0:T(8,128)(2,1)}), bf16[64,8,2048]{2,1,0:T(8,128)(2,1)}, u32[]{:S(2)}, u32[]{:S(2)}) async-start(bf16[64,8,2048]{2,1,0:T(8,128)(2,1)} %fusion.6), calls=%async_computation.2 | async-start | bytes 4194304 | tf_op jit(solution)/shard_map/all_to_all | solution.py:172
  (7 other events, 6.8 us)
Sparse Core Ops, SparseCore 0:
  41.1 40.0 all-gather.4
  82.8 62.4 all-gather.6
  157.8 31.0 reduce-scatter.1
where the time goes:
time: 284 us; the launch traced here: 283 us
  waiting for transfers between devices  123 us (43%)
  blocking collectives  53 us (19%)
  local copies, waits for them, and re-layouts  44.3 us (16%)
  matrix products  25.3 us (9%)
  other arithmetic  18.4 us (6%)
  between operations  13.6 us (5%)
  starting transfers between devices  5.34 us (2%)
    all_gather x1, waiting for transfers between devices, attention_block(): piece = lax.all_gather(cache_rows, 'seq', axis=0, tiled=True)  59.9 us
    all_to_all x1, blocking collectives, expert_block(): lax.all_to_all(copies, ('seq', 'expert'), split_axis=0, concat_axis=0, ti...  38.1 us
    reduce_scatter x1, waiting for transfers between devices, attention_block(): lax.psum_scatter(jnp.dot(spread, out_flat, preferred_element_type=jnp.flo...  30.2 us
    all_to_all x1, waiting for transfers between devices, expert_block(): lax.all_to_all(partial_value, ('seq', 'expert'), split_axis=0, concat_axi...  27.5 us
    all_gather x1, blocking collectives, attention_block(): gathered = lax.all_gather(own_rows, 'expert', axis=0, tiled=True)  15 us
    unnamed x57, local copies, waits for them, and re-layouts  11.2 us
    dot_general x2, local copies, waits for them, and re-layouts, attention_block(): jnp.dot(normed, query_weight.reshape(query_weight.shape[0], -1), preferre...  6.91 us
  transfers between devices with their start and end apart: 4, of which 4 were waited for; matrix products, arithmetic and copies ran while one was open for 14% of the time, Pallas kernels for 0%

commit v1 on v0

--- a/solution.py
+++ b/solution.py
@@ -57,7 +57,8 @@
 def attention_block(
     own_rows, lengths, cached, cache_rows, routes, gain, mixing, query_weight, kv_weight, out_weight
 ):
-    gathered = lax.all_gather(own_rows, "expert", axis=0, tiled=True)
+    sent = jnp.stack([own_rows] * lax.axis_size("expert"))
+    gathered = jnp.concatenate(lax.all_to_all(sent, "expert", 0, 0), axis=0)
     count = gathered.shape[0]
     normed = rms_scale(gathered, gain)
     row_index = lax.axis_index("seq") * count + jnp.arange(count, dtype=jnp.int32)

time: 284 us -> 273 us (0.961)
  blocking collectives: 53 us -> 37.9 us
  waiting for transfers between devices: 123 us -> 117 us
  starting transfers between devices: 5.34 us -> 11.3 us
  local copies, waits for them, and re-layouts: 44.3 us -> 49.7 us
    all_gather x1 -> x0, blocking collectives: 15 us -> none  [attention_block(): gathered = lax.all_gather(own_rows, 'expert', axis=0, tiled=True)]
    all_to_all x0 -> x1, starting transfers between devices: none -> 5.97 us  [attention_block(): gathered = jnp.concatenate(lax.all_to_all(sent, 'expert', 0, 0), axis=0)]
    all_gather x1, waiting for transfers between devices: 5.47 us -> 0.02 us  [attention_block(): piece = lax.all_gather(fresh, 'seq', axis=0, tiled=True)]
    unnamed x57 -> x41, local copies, waits for them, and re-layouts: 11.2 us -> 11.9 us
  transfers between devices with their start and end apart: 4 -> 5, of which waited for: 4 -> 3; matrix products, arithmetic and copies ran while one was open for 14% -> 21% of each run, Pallas kernels for 0% -> 0%
where the time goes in v1:
time: 273 us; the launch traced here: 272 us
  waiting for transfers between devices  117 us (43%)
  local copies, waits for them, and re-layouts  49.7 us (18%)
  blocking collectives  37.9 us (14%)
  matrix products  25.9 us (9%)
  other arithmetic  16.3 us (6%)
  between operations  13.6 us (5%)
  starting transfers between devices  11.3 us (4%)
    all_gather x1, waiting for transfers between devices, attention_block(): piece = lax.all_gather(cache_rows, 'seq', axis=0, tiled=True)  59.3 us
    all_to_all x1, blocking collectives, expert_block(): lax.all_to_all(copies, ('seq', 'expert'), split_axis=0, concat_axis=0, ti...  37.9 us
    reduce_scatter x1, waiting for transfers between devices, attention_block(): lax.psum_scatter(jnp.dot(spread, out_flat, preferred_element_type=jnp.flo...  30.4 us
    all_to_all x1, waiting for transfers between devices, expert_block(): lax.all_to_all(partial_value, ('seq', 'expert'), split_axis=0, concat_axi...  27.5 us
    unnamed x41, local copies, waits for them, and re-layouts  11.9 us
    dot_general x2, local copies, waits for them, and re-layouts, attention_block(): jnp.dot(normed, query_weight.reshape(query_weight.shape[0], -1), preferre...  7.73 us
    all_to_all x1, starting transfers between devices, attention_block(): gathered = jnp.concatenate(lax.all_to_all(sent, 'expert', 0, 0), axis=0)  5.97 us
    gather x10, local copies, waits for them, and re-layouts, route_gates(): chosen = jnp.take_along_axis(logits, routes, axis=1)  5.5 us
  transfers between devices with their start and end apart: 5, of which 3 were waited for; matrix products, arithmetic and copies ran while one was open for 21% of the time, Pallas kernels for 0%

profile of v1, /device:TPU:1, one launch (start us, length us, event | category | flops | bytes accessed | tf_op | source)
XLA Modules:
  0.0 272.0 jit_solution(5673191680287351649)
XLA Ops:
  8.4 6.0 %all-to-all-start = ((bf16[8,16,2048]{2,1,0:T(8,128)(2,1)}), bf16[8,16,2048]{2,1,0:T(8,128)(2,1)S(1)}, u32[]{:S(2)}, u32[]{:S(2)}) async-start(bf16[8,16,2048]{2,1,0:T(8,128)(2,1)} %stack.6), calls=%async_computation | async-start | bytes 1048576 | tf_op jit(solution)/shard_map/all_to_all | solution.py:61
  17.1 3.3 %copy.115 = bf16[256,8,2,256]{3,1,2,0:T(8,128)(2,1)} copy(bf16[256,8,2,256]{3,2,1,0:T(2,128)(2,1)} %bitcast.188) | data formatting | bytes 4194304
  20.5 4.0 %copy.97 = bf16[512,2048]{1,0:T(8,128)(2,1)} copy(bf16[512,2048]{0,1:T(8,128)(2,1)} %bitcast.183) | data formatting | bytes 4194304 | tf_op jit(solution)/shard_map/dot_general | solution.py:77
  25.9 2.3 fusion.97
  29.0 1.8 constant_dynamic-slice_fusion.1
  30.8 1.8 copy.113
  34.5 5.2 %copy.114 = bf16[256,8,4,256]{3,1,2,0:T(8,128)(2,1)} copy(bf16[256,8,4,256]{3,2,1,0:T(4,128)(2,1)} %bitcast.186) | data formatting | bytes 8388608
  39.7 6.5 %copy.89 = bf16[1024,2048]{1,0:T(8,128)(2,1)} copy(bf16[1024,2048]{0,1:T(8,128)(2,1)} %bitcast.179) | data formatting | bytes 8388608 | tf_op jit(solution)/shard_map/dot_general | solution.py:70
  52.4 1.8 broadcast_compare_fusion
  55.5 2.6 gather_fusion.1
  60.5 3.7 %fusion.96 = f32[128,4,2,128]{3,0,2,1:T(8,128)S(1)} fusion(bf16[128,2048,1,1]{1,0,3,2:T(8,128)(2,1)S(1)} %bitcast.185, bf16[4,2,128,2048]{3,2,1,0:T(8,128)(2,1)} %bitcast.178), kind=kOutput, calls=%fused_computation.167 | convolution fusion | flops 536870912 | bytes 5242880 | tf_op jit(solution)/shard_map/dot_general | solution.py:70
  65.5 2.3 gather_fusion.2
  70.7 2.1 fusion.94
  72.8 2.0 fusion.15
  74.8 59.3 %all-gather.6.cloned.1.call-done = bf16[1,2048,2,256]{1,3,2,0:T(8,128)(2,1)} async-done(((bf16[1,256,2,256]{1,3,2,0:T(8,128)(2,1)}), bf16[1,2048,2,256]{1,3,2,0:T(8,128)(2,1)}) %all-gather.6.cloned.1.call-update) | async-done | bytes 2097168 | tf_op jit(solution)/shard_map/all_gather | solution.py:111
  134.1 1.8 fusion.93
  142.9 3.7 %fusion.9 = bf16[128,2048]{1,0:T(8,128)(2,1)} fusion(bf16[4,256,2048]{2,1,0:T(8,128)(2,1)} %param.26, bf16[128,4,256]{2,1,0:T(4,128)(2,1)S(1)} %convolution_convert_fusion.2), kind=kOutput, calls=%fused_computation.16 | convolution fusion | flops 537133056 | bytes 4980736 | tf_op jit(solution)/shard_map/dot_general | solution.py:132
  147.4 30.4 %reduce-scatter.2.cloned.1.call-done = bf16[16,2048]{1,0:T(8,128)(2,1)} async-done(((bf16[128,2048]{1,0:T(8,128)(2,1)}), bf16[16,2048]{1,0:T(8,128)(2,1)}) %reduce-scatter.2.cloned.1.call-update) | async-done | bytes 65552 | tf_op jit(solution)/shard_map/reduce_scatter | solution.py:131
  179.4 37.9 %all_to_all.15 = bf16[64,8,2048]{2,1,0:T(8,128)(2,1)S(1)} all-to-all(bf16[64,8,2048]{2,1,0:T(8,128)(2,1)S(1)} %bitcast.182), channel_id=1, replica_groups=mesh['section'=2,'seq'=8,'expert'=8] {'seq','expert'}, dimensions={0} | all-to-all | bytes 4194304 | tf_op jit(solution)/shard_map/all_to_all | solution.py:168
  217.3 5.2 %fusion = f32[512,2,704]{0,2,1:T(8,128)S(1)} fusion(bf16[1,2048,2,704]{1,3,2,0:T(8,128)(2,1)} %param.28, bf16[64,8,2048]{2,1,0:T(8,128)(2,1)S(1)} %all_to_all.15), kind=kOutput, calls=%fused_computation.4 | convolution fusion | flops 2952790016 | bytes 10747904 | tf_op jit(solution)/shard_map/dot_general | solution.py:142
  222.6 3.3 %fusion.6 = bf16[64,8,2048]{2,1,0:T(8,128)(2,1)} fusion(bf16[1,704,2048]{2,1,0:T(8,128)(2,1)S(1)} %copy-done, f32[512,2,704]{0,2,1:T(8,128)S(1)} %fusion), kind=kOutput, calls=%fused_computation.14 | convolution fusion | flops 1479606272 | bytes 7864320 | tf_op jit(solution)/shard_map/dot_general | solution.py:171
  225.9 5.3 %all-to-all-start.2 = ((bf16[64,8,2048]{2,1,0:T(8,128)(2,1)}), bf16[64,8,2048]{2,1,0:T(8,128)(2,1)}, u32[]{:S(2)}, u32[]{:S(2)}) async-start(bf16[64,8,2048]{2,1,0:T(8,128)(2,1)} %fusion.6), calls=%async_computation.3 | async-start | bytes 4194304 | tf_op jit(solution)/shard_map/all_to_all | solution.py:173
  232.6 27.5 %all-to-all-done.2 = bf16[64,8,2048]{2,1,0:T(8,128)(2,1)} async-done(((bf16[64,8,2048]{2,1,0:T(8,128)(2,1)}), bf16[64,8,2048]{2,1,0:T(8,128)(2,1)}, u32[]{:S(2)}, u32[]{:S(2)}) %all-to-all-start.2) | async-done | bytes 2097184 | tf_op jit(solution)/shard_map/all_to_all | solution.py:173
  260.1 2.0 convert_reduce_fusion
  (133 shorter events, 36.4 us)
Async XLA Ops:
  6.5 216.0 %copy-start = (bf16[1,704,2048]{2,1,0:T(8,128)(2,1)S(1)}, bf16[1,704,2048]{2,1,0:T(8,128)(2,1)}, u32[]{:S(2)}) copy-start(bf16[1,704,2048]{2,1,0:T(8,128)(2,1)} %param.29) | copy-start | bytes 8650756
  8.4 16.3 %all-to-all-start = ((bf16[8,16,2048]{2,1,0:T(8,128)(2,1)}), bf16[8,16,2048]{2,1,0:T(8,128)(2,1)S(1)}, u32[]{:S(2)}, u32[]{:S(2)}) async-start(bf16[8,16,2048]{2,1,0:T(8,128)(2,1)} %stack.6), calls=%async_computation | async-start | bytes 1048576 | tf_op jit(solution)/shard_map/all_to_all | solution.py:61
  14.3 56.4 %all-gather.4.cloned.1.call-start = ((), (), s32[]{:S(2)}) async-start(), calls=%async_computation.4 | async-start | bytes 1179648 | tf_op jit(solution)/shard_map/all_gather | solution.py:115
  15.7 4.7 %copy-start.15 = (s32[3,1]{0,1:T(1,128)}, s32[3,1]{0,1:T(1,128)S(1)}, u32[]{:S(2)}) copy-start(s32[3,1]{0,1:T(1,128)S(1)} %reduce-window.13) | copy-start | bytes 40
  16.4 0.7 copy-start.16
  16.5 0.5 copy-start.13
  20.5 4.4 %copy-start.10 = (f32[2048]{0:T(1024)S(1)}, f32[2048]{0:T(1024)}, u32[]{:S(2)}) copy-start(f32[2048]{0:T(1024)} %param.21) | copy-start | bytes 24580
  25.1 0.8 copy-start.2
  29.0 105.1 %all-gather.6.cloned.1.call-start = ((), (), s32[]{:S(2)}) async-start(), calls=%async_computation.6 | async-start | bytes 2359296 | tf_op jit(solution)/shard_map/all_gather | solution.py:111
  32.7 145.2 %reduce-scatter.2.cloned.1.call-start = ((), (), s32[]{:S(2)}) async-start(), calls=%async_computation.5 | async-start | bytes 589824 | tf_op jit(solution)/shard_map/reduce_scatter | solution.py:131
  55.5 4.3 %copy-start.14 = (s32[2,128,2]{1,2,0:T(2,128)S(1)}, s32[2,128,2]{1,2,0:T(2,128)}, u32[]{:S(2)}) copy-start(s32[2,128,2]{1,2,0:T(2,128)} %param.19) | copy-start | bytes 6148
  55.5 5.0 %copy-start.3 = (bf16[8,16,2048]{2,1,0:T(8,128)(2,1)S(1)}, bf16[8,16,2048]{2,1,0:T(8,128)(2,1)}, u32[]{:S(2)}) copy-start(bf16[8,16,2048]{2,1,0:T(8,128)(2,1)} %copy-done.2) | copy-start | bytes 1572868
  64.2 6.0 %copy-start.7 = (f32[128,64]{1,0:T(8,128)S(1)}, f32[128,64]{1,0:T(8,128)}, u32[]{:S(2)}) copy-start(f32[128,64]{1,0:T(8,128)} %copy.93) | copy-start | bytes 98308
  65.5 7.4 %copy-start.5 = (pred[256,1024]{1,0:T(8,128)(4,1)S(1)}, pred[256,1024]{1,0:T(8,128)(4,1)}, u32[]{:S(2)}) copy-start(pred[256,1024]{1,0:T(8,128)(4,1)} %fusion.37) | copy-start | bytes 786436
  134.1 1.8 copy-start.4
  137.2 1.6 copy-start.1
  139.6 1.5 copy-start.6
  141.1 1.1 copy-start.9
  141.1 1.1 copy-start.11
  142.9 3.8 %copy-start.17 = (s32[2,16,2]{1,2,0:T(2,128)S(1)}, s32[2,16,2]{1,2,0:T(2,128)}, u32[]{:S(2)}) copy-start(s32[2,16,2]{1,2,0:T(2,128)} %param.20) | copy-start | bytes 772
  142.9 35.0 %copy-start.8 = (bf16[2,16,2048]{2,1,0:T(8,128)(2,1)S(1)}, bf16[2,16,2048]{2,1,0:T(8,128)(2,1)}, u32[]{:S(2)}) copy-start(bf16[2,16,2048]{2,1,0:T(8,128)(2,1)} %param.15) | copy-start | bytes 393220
  142.9 36.0 %copy-start.12 = (f32[2048]{0:T(1024)S(1)}, f32[2048]{0:T(1024)}, u32[]{:S(2)}) copy-start(f32[2048]{0:T(1024)} %param.22) | copy-start | bytes 24580
  225.9 5.7 %copy-start.18 = (bf16[2048,8]{0,1:T(8,128)(2,1)S(1)}, bf16[2048,8]{0,1:T(8,128)(2,1)}, u32[]{:S(2)}) copy-start(bf16[2048,8]{0,1:T(8,128)(2,1)} %param.27) | copy-start | bytes 98308
  225.9 34.2 %all-to-all-start.2 = ((bf16[64,8,2048]{2,1,0:T(8,128)(2,1)}), bf16[64,8,2048]{2,1,0:T(8,128)(2,1)}, u32[]{:S(2)}, u32[]{:S(2)}) async-start(bf16[64,8,2048]{2,1,0:T(8,128)(2,1)} %fusion.6), calls=%async_computation.3 | async-start | bytes 4194304 | tf_op jit(solution)/shard_map/all_to_all | solution.py:173
Sparse Core Ops, SparseCore 0:
  29.1 41.0 all-gather.3
  71.7 62.3 all-gather.5
  146.8 31.0 reduce-scatter.1
